TPU v7x, 32 devices: a whole 2x2x4 slice. The times are simulated.
32 devices in a mesh: pb: 4 (over y, core), kv: 8 (over z, x).
Axes of the slice: x: 2, y: 2, z: 4, core: 2. Of those that a mesh axis runs over, the one named last changes fastest.
Arguments:
- queries: bfloat16 [8192, 128], P(('pb', 'kv')), may hold values from -15 to 15
- query_tangent: bfloat16 [8192, 128], P(('pb', 'kv')), may hold values from -2 to 2
- keys: bfloat16 [8192, 128], P(('pb', 'kv')), may hold values from -8 to 8
- values: bfloat16 [8192, 128], P(('pb', 'kv')), may hold values from -6 to 6
- key_tangent: bfloat16 [8192, 128], P(('pb', 'kv')), may hold values from -2 to 2
- value_tangent: bfloat16 [8192, 128], P(('pb', 'kv')), may hold values from -6 to 6
- block_list: int32 [64, 8, 8], P('pb', 'kv'), may hold values from 0 to 63, as said below
- block_count: int32 [64, 8], P('pb', 'kv'), may hold values from 1 to 8, as said below
Outputs:
- attended: bfloat16 [8192, 128], P(('pb', 'kv'))
- attended_tangent: bfloat16 [8192, 128], P(('pb', 'kv'))
Inputs may be any that keep to these rules, and one draw needn't show every extreme that they name: `block_list`: entries for one query block and slab j are distinct key blocks g whose index g // (256 // 128) leaves remainder j when divided by 8; entries past block_count are valid but unused. `block_count`: the value 8 is reached in every key slab.
All inputs are finite; a program needn't handle non-finite values.
Results may differ from a plain program's by a relative error of at most 0.01.
Values may be sent and summed in bfloat16 or wider, within the bound.
A program may use at most 128 MiB of HBM per device.

v0:
```python
import math
import jax
import jax.numpy as jnp
from jax import lax
from jax.sharding import PartitionSpec as P

BLK = 128
LMAX = 8


def shards(
    queries, query_tangent, keys, values, key_tangent, value_tangent, block_list, block_count
):
    head_dim = queries.shape[1]
    shard_rows = keys.shape[0]
    shard_blocks = shard_rows // BLK
    slab_count = lax.axis_size("kv")
    score_scale = 1.0 / math.sqrt(head_dim)
    query_all, qtangent_all = (
        lax.all_gather(queries, "kv", axis=0, tiled=True),
        lax.all_gather(query_tangent, "kv", axis=0, tiled=True),
    )
    key_all, value_all, ktangent_all, vtangent_all = (
        lax.all_gather(keys, "pb", axis=0, tiled=True),
        lax.all_gather(values, "pb", axis=0, tiled=True),
        lax.all_gather(key_tangent, "pb", axis=0, tiled=True),
        lax.all_gather(value_tangent, "pb", axis=0, tiled=True),
    )
    key_blocks = key_all.reshape(-1, BLK, head_dim)
    value_blocks = value_all.reshape(-1, BLK, head_dim)
    keyt_blocks = ktangent_all.reshape(-1, BLK, head_dim)
    valuet_blocks = vtangent_all.reshape(-1, BLK, head_dim)
    global_ids = block_list[:, 0, :]
    shard_id = global_ids // shard_blocks
    local_index = shard_id // slab_count * shard_blocks + global_ids % shard_blocks
    counts_all = block_count[:, 0]
    query_blocks = query_all.shape[0] // BLK
    group_size = 8
    groups = query_blocks // group_size

    def attend(items):
        query_group, tangent_group, picked, counts = items
        flat = picked.reshape(-1)
        key_rows = key_blocks[flat].reshape(group_size, -1, head_dim)
        value_rows = value_blocks[flat].reshape(group_size, -1, head_dim)
        keyt_rows = keyt_blocks[flat].reshape(group_size, -1, head_dim)
        valuet_rows = valuet_blocks[flat].reshape(group_size, -1, head_dim)
        active = jnp.repeat(jnp.arange(LMAX)[None, :] < counts[:, None], BLK, axis=1)
        scores = (
            jnp.einsum("gqd,gkd->gqk", query_group, key_rows, preferred_element_type=jnp.float32)
            * score_scale
        )
        score_tangent = (
            jnp.einsum("gqd,gkd->gqk", tangent_group, key_rows, preferred_element_type=jnp.float32)
            + jnp.einsum("gqd,gkd->gqk", query_group, keyt_rows, preferred_element_type=jnp.float32)
        ) * score_scale
        peak = jnp.max(jnp.where(active[:, None, :], scores, -jnp.inf), axis=2)
        weights = jnp.where(active[:, None, :], jnp.exp(scores - peak[:, :, None]), 0.0)
        total = jnp.sum(weights, axis=2)
        slope = jnp.sum(weights * score_tangent, axis=2)
        weights_b = weights.astype(jnp.bfloat16)
        scaled_b = (weights * score_tangent).astype(jnp.bfloat16)
        weighted = jnp.einsum(
            "gqk,gkd->gqd", weights_b, value_rows, preferred_element_type=jnp.float32
        )
        tangent_sum = jnp.einsum(
            "gqk,gkd->gqd", scaled_b, value_rows, preferred_element_type=jnp.float32
        ) + jnp.einsum("gqk,gkd->gqd", weights_b, valuet_rows, preferred_element_type=jnp.float32)
        return (peak, total, weighted, slope, tangent_sum)

    peak, total, weighted, slope, tangent_sum = lax.map(
        attend,
        (
            query_all.reshape(groups, group_size, BLK, head_dim),
            qtangent_all.reshape(groups, group_size, BLK, head_dim),
            local_index.reshape(groups, group_size, LMAX),
            counts_all.reshape(groups, group_size),
        ),
    )
    slab_rows = query_all.shape[0]
    peak = peak.reshape(slab_rows)
    total = total.reshape(slab_rows)
    slope = slope.reshape(slab_rows)
    weighted = weighted.reshape(slab_rows, head_dim)
    tangent_sum = tangent_sum.reshape(slab_rows, head_dim)
    peak_all = lax.pmax(peak, "kv")
    factor = jnp.exp(peak - peak_all)
    total_own, weighted_own, slope_own, tangent_own = (
        lax.psum_scatter(total * factor, "kv", scatter_dimension=0, tiled=True),
        lax.psum_scatter(weighted * factor[:, None], "kv", scatter_dimension=0, tiled=True),
        lax.psum_scatter(slope * factor, "kv", scatter_dimension=0, tiled=True),
        lax.psum_scatter(tangent_sum * factor[:, None], "kv", scatter_dimension=0, tiled=True),
    )
    output = weighted_own / total_own[:, None]
    output_tangent = tangent_own / total_own[:, None] - (slope_own / total_own)[:, None] * output
    return (output.astype(jnp.bfloat16), output_tangent.astype(jnp.bfloat16))


def solution(mesh):
    in_specs = (
        P(("pb", "kv"), None),
        P(("pb", "kv"), None),
        P(("pb", "kv"), None),
        P(("pb", "kv"), None),
        P(("pb", "kv"), None),
        P(("pb", "kv"), None),
        P("pb", "kv", None),
        P("pb", "kv"),
    )
    out_specs = (P(("pb", "kv"), None), P(("pb", "kv"), None))
    return jax.shard_map(shards, mesh=mesh, in_specs=in_specs, out_specs=out_specs, check_vma=False)
```

profile of v0, /device:TPU:0, one launch (start us, length us, event | category | flops | bytes accessed | tf_op | source)
XLA Modules:
  0.0 322.6 jit_solution(14211954801585777682)
XLA Ops:
  7.3 0.5 broadcast.93
  7.8 1.3 reduce.3
  9.1 0.1 reshape_squeeze.3
  9.2 35.4 %all_gather.18 = bf16[2048,128]{1,0:T(8,128)(2,1)} all-gather(bf16[256,128]{1,0:T(8,128)(2,1)} %param.10), channel_id=1, replica_groups=mesh['pb'=4,'kv'=8] {'kv'}, dimensions={0}, use_global_device_ids=true | all-gather | bytes 589824 | tf_op jit(solution)/shard_map/all_gather | solution.py:20
  44.6 33.6 %all_gather.21 = bf16[2048,128]{1,0:T(8,128)(2,1)} all-gather(bf16[256,128]{1,0:T(8,128)(2,1)} %param.11), channel_id=1, replica_groups=mesh['pb'=4,'kv'=8] {'kv'}, dimensions={0}, use_global_device_ids=true | all-gather | bytes 589824 | tf_op jit(solution)/shard_map/all_gather | solution.py:21
  78.2 6.0 %all_gather.19 = bf16[1024,128]{1,0:T(8,128)(2,1)S(1)} all-gather(bf16[256,128]{1,0:T(8,128)(2,1)} %param.12), channel_id=1, replica_groups=mesh['pb'=4,'kv'=8] {'pb'}, dimensions={0}, use_global_device_ids=true | all-gather | bytes 327680 | tf_op jit(solution)/shard_map/all_gather | solution.py:24
  84.2 6.0 %all_gather.20 = bf16[1024,128]{1,0:T(8,128)(2,1)S(1)} all-gather(bf16[256,128]{1,0:T(8,128)(2,1)} %param.13), channel_id=1, replica_groups=mesh['pb'=4,'kv'=8] {'pb'}, dimensions={0}, use_global_device_ids=true | all-gather | bytes 327680 | tf_op jit(solution)/shard_map/all_gather | solution.py:25
  90.2 6.0 %all_gather.22 = bf16[1024,128]{1,0:T(8,128)(2,1)S(1)} all-gather(bf16[256,128]{1,0:T(8,128)(2,1)} %param.14), channel_id=1, replica_groups=mesh['pb'=4,'kv'=8] {'pb'}, dimensions={0}, use_global_device_ids=true | all-gather | bytes 327680 | tf_op jit(solution)/shard_map/all_gather | solution.py:26
  96.3 6.0 %all_gather.23 = bf16[1024,128]{1,0:T(8,128)(2,1)S(1)} all-gather(bf16[256,128]{1,0:T(8,128)(2,1)} %param.15), channel_id=1, replica_groups=mesh['pb'=4,'kv'=8] {'pb'}, dimensions={0}, use_global_device_ids=true | all-gather | bytes 327680 | tf_op jit(solution)/shard_map/all_gather | solution.py:27
  102.3 0.8 squeeze.14
  103.2 57.1 %while.18 = (s32[]{:T(128)}, f32[2,8,128]{2,1,0:T(8,128)S(1)}, f32[2,8,128]{2,1,0:T(8,128)S(1)}, f32[2,8,128,128]{3,2,1,0:T(8,128)}, f32[2,8,128]{2,1,0:T(8,128)...) while((s32[]{:T(128)}, f32[2,8,128]{2,1,0:T(8,128)S(1)}, ...), condition=%wide.region_4.5_spmd, body=%wide.region_0.4_spmd.sunk | while | flops 1634859264 | bytes 101561608 | solution.py:71
  103.2 0.1 reshape.163
  103.3 1.0 gather_fusion
  104.3 0.1 broadcast_bitcast_fusion.2
  104.4 3.6 %select_reduce_fusion.2 = (f32[8,128]{1,0:T(8,128)S(1)}, f32[8,128,1024]{2,1,0:T(8,128)}) fusion(pred[8,1024]{1,0:T(8,128)(4,1)S(1)} %broadcast_bitcast_fusion.2, bf16[8,1024,128]{2,1,0:T(8,128)(2,1)S(1)} %bitcast.106, bf16[2,8,128,128]{3,2,1,0:T(8,128)(2,1)} %get-tuple-element.291, s32[]{:T(128)} %get-tuple-element.269), kind=kOutput, calls=%fused_computation.6.clone.1 | convolution fusion | flops 271580160 | bytes 6566400 | tf_op jit(solution)/shard_map/while/body/eval_jaxpr/gqd,gkd->gqk/dot_general | solution.py:50
  108.1 2.7 fusion.66
  110.7 2.2 gather_fusion.1
  112.9 5.8 %fusion.67 = (f32[8,128]{1,0:T(8,128)S(1)}, bf16[8,128,1024]{2,1,0:T(8,128)(2,1)S(1)}) fusion(f32[8,128,1024]{2,1,0:T(8,128)} %fusion.66, bf16[8,1024,128]{2,1,0:T(8,128)(2,1)} %bitcast.112, bf16[2,8,128,128]{3,2,1,0:T(8,128)(2,1)} %get-tuple-element.291, s32[]{:T(128)} %get-tuple-element.269, f32[8,128]{1,0:T(8,128)S(1)} %get-tuple-element.248, ...), kind=kOutput, calls=%fused_computation.61.clone.1 | convolution fusion | flops 276823040 | bytes 12861952 | tf_op jit(solution)/shard_map/while/body/eval_jaxpr/gqd,gkd->gqk/dot_general | solution.py:55
  118.7 2.1 gather_fusion.2
  120.8 3.1 fusion.70
  123.9 0.9 gather_fusion.3
  124.9 4.3 %fusion.71 = f32[2,8,128,128]{3,2,1,0:T(8,128)} fusion(f32[2,8,128,128]{3,2,1,0:T(8,128)} %get-tuple-element.274, s32[]{:T(128)} %get-tuple-element.269, f32[8,128,128]{2,1,0:T(8,128)} %fusion.70, bf16[8,1024,128]{2,1,0:T(8,128)(2,1)S(1)} %bitcast.115, f32[8,128,1024]{2,1,0:T(8,128)} %get-tuple-element.249, f32[8,128]{1,0:T(8,128)S(1)} %get-tuple-element.248, ...), kind=kOutput, calls=%fused_computation.15.clone.1 | convolution fusion | flops 272760832 | bytes 7352832 | tf_op jit(solution)/shard_map/while/body/eval_jaxpr/gqk,gkd->gqd/dot_general | solution.py:68
  129.2 0.4 copy-done.3
  129.6 1.0 fusion.69
  130.6 1.1 fusion.68
  131.8 0.1 reshape.163
  131.9 1.0 gather_fusion
  132.9 0.1 broadcast_bitcast_fusion.2
  133.0 3.6 %select_reduce_fusion.2 = (f32[8,128]{1,0:T(8,128)S(1)}, f32[8,128,1024]{2,1,0:T(8,128)}) fusion(pred[8,1024]{1,0:T(8,128)(4,1)S(1)} %broadcast_bitcast_fusion.2, bf16[8,1024,128]{2,1,0:T(8,128)(2,1)S(1)} %bitcast.106, bf16[2,8,128,128]{3,2,1,0:T(8,128)(2,1)} %get-tuple-element.291, s32[]{:T(128)} %get-tuple-element.269), kind=kOutput, calls=%fused_computation.6.clone.1 | convolution fusion | flops 271580160 | bytes 6566400 | tf_op jit(solution)/shard_map/while/body/eval_jaxpr/gqd,gkd->gqk/dot_general | solution.py:50
  136.6 2.7 fusion.66
  139.3 2.2 gather_fusion.1
  141.5 5.7 %fusion.67 = (f32[8,128]{1,0:T(8,128)S(1)}, bf16[8,128,1024]{2,1,0:T(8,128)(2,1)S(1)}) fusion(f32[8,128,1024]{2,1,0:T(8,128)} %fusion.66, bf16[8,1024,128]{2,1,0:T(8,128)(2,1)} %bitcast.112, bf16[2,8,128,128]{3,2,1,0:T(8,128)(2,1)} %get-tuple-element.291, s32[]{:T(128)} %get-tuple-element.269, f32[8,128]{1,0:T(8,128)S(1)} %get-tuple-element.248, ...), kind=kOutput, calls=%fused_computation.61.clone.1 | convolution fusion | flops 276823040 | bytes 12861952 | tf_op jit(solution)/shard_map/while/body/eval_jaxpr/gqd,gkd->gqk/dot_general | solution.py:55
  147.3 2.1 gather_fusion.2
  149.4 3.1 fusion.70
  152.5 0.9 gather_fusion.3
  153.5 4.3 %fusion.71 = f32[2,8,128,128]{3,2,1,0:T(8,128)} fusion(f32[2,8,128,128]{3,2,1,0:T(8,128)} %get-tuple-element.274, s32[]{:T(128)} %get-tuple-element.269, f32[8,128,128]{2,1,0:T(8,128)} %fusion.70, bf16[8,1024,128]{2,1,0:T(8,128)(2,1)S(1)} %bitcast.115, f32[8,128,1024]{2,1,0:T(8,128)} %get-tuple-element.249, f32[8,128]{1,0:T(8,128)S(1)} %get-tuple-element.248, ...), kind=kOutput, calls=%fused_computation.15.clone.1 | convolution fusion | flops 272760832 | bytes 7352832 | tf_op jit(solution)/shard_map/while/body/eval_jaxpr/gqk,gkd->gqd/dot_general | solution.py:68
  157.8 0.4 copy-done.3
  158.1 1.0 fusion.69
  159.2 1.1 fusion.68
  160.3 21.9 %pmax.7 = f32[2048]{0:T(1024)S(1)} all-reduce(f32[2048]{0:T(1024)S(1)} %bitcast.118), channel_id=1, replica_groups=mesh['pb'=4,'kv'=8] {'kv'}, use_global_device_ids=true, to_apply=%region_5.6 | all-reduce | flops 2048 | bytes 16384 | tf_op jit(solution)/shard_map/pmax | solution.py:86
  182.3 3.2 %bitcast_multiply_fusion = (f32[2048,128]{1,0:T(8,128)}, f32[2048,128]{1,0:T(8,128)}) fusion(f32[2,8,128,128]{3,2,1,0:T(8,128)} %get-tuple-element.81, f32[2048]{0:T(1024)S(1)} %get-tuple-element.144, f32[2,8,128,128]{3,2,1,0:T(8,128)} %get-tuple-element.78), kind=kLoop, calls=%fused_computation.42 | loop fusion | flops 524288 | bytes 4202496 | tf_op jit(solution)/shard_map/mul | solution.py:92
  185.6 0.7 reduce-scatter.5.cloned.1.call-update
  186.3 0.6 dynamic-slice
  187.5 33.1 %all-reduce.2 = (f32[2048]{0:T(1024)S(1)}, f32[2048]{0:T(1024)S(1)}) all-reduce(f32[2048]{0:T(1024)S(1)} %bitcast_multiply_fusion.3, f32[2048]{0:T(1024)S(1)} %get-tuple-element.143), channel_id=3, replica_groups=mesh['pb'=4,'kv'=8] {'kv'}, use_global_device_ids=true, to_apply=%region_7.8.clone | all-reduce | flops 4096 | bytes 32768
  220.6 0.1 dynamic-slice_divide_fusion
  220.7 26.4 %reduce-scatter.3.cloned.1.call-done = f32[256,128]{1,0:T(8,128)} async-done(((f32[2048,128]{1,0:T(8,128)}), f32[256,128]{1,0:T(8,128)}) %reduce-scatter.3.cloned.1.call-update) | async-done | bytes 131088 | tf_op jit(solution)/shard_map/reduce_scatter | solution.py:90
  247.1 66.9 %reduce-scatter.5.cloned.1.call-done = f32[256,128]{1,0:T(8,128)} async-done(((f32[2048,128]{1,0:T(8,128)}), f32[256,128]{1,0:T(8,128)}) %reduce-scatter.5.cloned.1.call-update) | async-done | bytes 131088 | tf_op jit(solution)/shard_map/reduce_scatter | solution.py:92
  314.0 1.7 subtract_convert_fusion
  (47 shorter events, 0.5 us)
Async XLA Ops:
  7.2 239.9 %reduce-scatter.3.cloned.1.call-start = ((), (), s32[]{:S(2)}) async-start(), calls=%async_computation.2 | async-start | bytes 1179648 | tf_op jit(solution)/shard_map/reduce_scatter | solution.py:90
  104.3 3.7 %copy-start.2 = (bf16[2,8,128,128]{3,2,1,0:T(8,128)(2,1)S(1)}, bf16[2,8,128,128]{3,2,1,0:T(8,128)(2,1)}, u32[]{:S(2)}) copy-start(bf16[2,8,128,128]{3,2,1,0:T(8,128)(2,1)} %get-tuple-element.295) | copy-start | bytes 1572868 | tf_op jit(solution)/shard_map/while
  124.9 4.3 %copy-start = (f32[8,128,1024]{2,1,0:T(8,128)S(1)}, f32[8,128,1024]{2,1,0:T(8,128)}, u32[]{:S(2)}) copy-start(f32[8,128,1024]{2,1,0:T(8,128)} %get-tuple-element.249) | copy-start | bytes 12582916 | tf_op jit(solution)/shard_map/while
  124.9 4.3 %copy-start.1 = (bf16[64,128,128]{2,1,0:T(8,128)(2,1)S(1)}, bf16[64,128,128]{2,1,0:T(8,128)(2,1)}, u32[]{:S(2)}) copy-start(bf16[64,128,128]{2,1,0:T(8,128)(2,1)} %gather_fusion.2) | copy-start | bytes 6291460 | tf_op jit(solution)/shard_map/while
  124.9 4.7 %copy-start.3 = (f32[2,8,128,128]{3,2,1,0:T(8,128)S(1)}, f32[2,8,128,128]{3,2,1,0:T(8,128)}, u32[]{:S(2)}) copy-start(f32[2,8,128,128]{3,2,1,0:T(8,128)} %get-tuple-element.272) | copy-start | bytes 3145732 | tf_op jit(solution)/shard_map/while
  130.6 1.1 copy-start.4
  132.9 3.7 %copy-start.2 = (bf16[2,8,128,128]{3,2,1,0:T(8,128)(2,1)S(1)}, bf16[2,8,128,128]{3,2,1,0:T(8,128)(2,1)}, u32[]{:S(2)}) copy-start(bf16[2,8,128,128]{3,2,1,0:T(8,128)(2,1)} %get-tuple-element.295) | copy-start | bytes 1572868 | tf_op jit(solution)/shard_map/while
  153.5 4.3 %copy-start = (f32[8,128,1024]{2,1,0:T(8,128)S(1)}, f32[8,128,1024]{2,1,0:T(8,128)}, u32[]{:S(2)}) copy-start(f32[8,128,1024]{2,1,0:T(8,128)} %get-tuple-element.249) | copy-start | bytes 12582916 | tf_op jit(solution)/shard_map/while
  153.5 4.3 %copy-start.1 = (bf16[64,128,128]{2,1,0:T(8,128)(2,1)S(1)}, bf16[64,128,128]{2,1,0:T(8,128)(2,1)}, u32[]{:S(2)}) copy-start(bf16[64,128,128]{2,1,0:T(8,128)(2,1)} %gather_fusion.2) | copy-start | bytes 6291460 | tf_op jit(solution)/shard_map/while
  153.5 4.7 %copy-start.3 = (f32[2,8,128,128]{3,2,1,0:T(8,128)S(1)}, f32[2,8,128,128]{3,2,1,0:T(8,128)}, u32[]{:S(2)}) copy-start(f32[2,8,128,128]{3,2,1,0:T(8,128)} %get-tuple-element.272) | copy-start | bytes 3145732 | tf_op jit(solution)/shard_map/while
  159.1 1.1 copy-start.4
  160.3 26.0 %copy-start.5 = (u32[32]{0:T(128)S(1)}, u32[32]{0:T(128)}, u32[]{:S(2)}) copy-start(u32[32]{0:T(128)} %constant.74) | copy-start | bytes 388
  185.5 128.5 %reduce-scatter.5.cloned.1.call-start = ((), (), s32[]{:S(2)}) async-start(), calls=%async_computation.3 | async-start | bytes 1179648 | tf_op jit(solution)/shard_map/reduce_scatter | solution.py:92
Sparse Core Ops, SparseCore 0:
  185.6 61.3 reduce-scatter.2
  250.5 63.4 reduce-scatter.4
where the time goes:
time: 323 us
  blocking collectives  148 us (46%)
  waiting for transfers between devices  94 us (29%)
  matrix products  40.8 us (13%)
  local copies, waits for them, and re-layouts  15.8 us (5%)
  between operations  14.8 us (5%)
  other arithmetic  8.65 us (3%)
    reduce_scatter x1, waiting for transfers between devices, shards(): lax.psum_scatter(tangent_sum * factor[:, None], 'kv', scatter_dimension=0...  66.9 us
    all_gather x1, blocking collectives, shards(): lax.all_gather(queries, 'kv', axis=0, tiled=True)  35.4 us
    all_gather x1, blocking collectives, shards(): lax.all_gather(query_tangent, 'kv', axis=0, tiled=True)  33.6 us
    unnamed x1, blocking collectives  33.1 us
    reduce_scatter x1, waiting for transfers between devices, shards(): lax.psum_scatter(weighted * factor[:, None], 'kv', scatter_dimension=0, t...  26.4 us
    pmax x1, blocking collectives, shards(): peak_all = lax.pmax(peak, 'kv')  21.9 us
    dot_general x2, matrix products, attend(): jnp.einsum('gqd,gkd->gqk', query_group, keyt_rows, preferred_element_type...  11.5 us
    dot_general x2, matrix products, attend(): jnp.einsum('gqk,gkd->gqd', weights_b, valuet_rows, preferred_element_type...  8.55 us
  transfers between devices with their start and end apart: 2, of which 2 were waited for; matrix products, arithmetic and copies ran while one was open for 0% of the time, Pallas kernels for 0%

commit v1 on v0

--- a/solution.py
+++ b/solution.py
@@ -6,6 +6,27 @@
 
 BLK = 128
 LMAX = 8
+
+
+def laid_out(pieces, dim):
+    pieces = jnp.moveaxis(pieces, 0, dim)
+    lengths = pieces.shape
+    return pieces.reshape(*lengths[:dim], lengths[dim] * lengths[dim + 1], *lengths[dim + 2 :])
+
+
+def grow_blocks(shard, axis):
+    devices, index = (lax.axis_size(axis), lax.axis_index(axis))
+    pieces, bit = (shard[None], 1)
+    while bit < devices:
+        other = lax.ppermute(pieces, axis, [(i, i ^ bit) for i in range(devices)])
+        low = index & bit == 0
+        pieces = jnp.concatenate([jnp.where(low, pieces, other), jnp.where(low, other, pieces)])
+        bit *= 2
+    return pieces
+
+
+def doubled_up(value, axis, dim):
+    return laid_out(grow_blocks(value, axis), dim)
 
 
 def shards(
@@ -18,7 +39,7 @@
     score_scale = 1.0 / math.sqrt(head_dim)
     query_all, qtangent_all = (
         lax.all_gather(queries, "kv", axis=0, tiled=True),
-        lax.all_gather(query_tangent, "kv", axis=0, tiled=True),
+        doubled_up(query_tangent, "kv", 0),
     )
     key_all, value_all, ktangent_all, vtangent_all = (
         lax.all_gather(keys, "pb", axis=0, tiled=True),

time: 323 us -> 293 us (0.907)
  blocking collectives: 148 us -> 110 us
  starting transfers between devices: 0.08 us -> 7.41 us
    all_gather x1 -> x0, blocking collectives: 33.6 us -> none  [shards(): lax.all_gather(query_tangent, 'kv', axis=0, tiled=True)]
    ppermute x0 -> x3, starting transfers between devices: none -> 7.33 us  [grow_blocks(): other = lax.ppermute(pieces, axis, [(i, i ^ bit) for i in range(devices)])]
    pmax x1, blocking collectives: 21.9 us -> 17.7 us  [shards(): peak_all = lax.pmax(peak, 'kv')]
  transfers between devices with their start and end apart: 2 -> 5, of which waited for: 2 -> 2; matrix products, arithmetic and copies ran while one was open for 0% -> 1% of each run, Pallas kernels for 0% -> 0%
where the time goes in v1:
time: 293 us
  blocking collectives  110 us (38%)
  waiting for transfers between devices  93.1 us (32%)
  matrix products  40.8 us (14%)
  local copies, waits for them, and re-layouts  15.7 us (5%)
  between operations  14.8 us (5%)
  other arithmetic  10.5 us (4%)
  starting transfers between devices  7.41 us (3%)
    reduce_scatter x1, waiting for transfers between devices, shards(): lax.psum_scatter(tangent_sum * factor[:, None], 'kv', scatter_dimension=0...  66.5 us
    unnamed x1, blocking collectives  34.9 us
    all_gather x1, blocking collectives, shards(): lax.all_gather(queries, 'kv', axis=0, tiled=True)  33.6 us
    reduce_scatter x1, waiting for transfers between devices, shards(): lax.psum_scatter(weighted * factor[:, None], 'kv', scatter_dimension=0, t...  25.9 us
    pmax x1, blocking collectives, shards(): peak_all = lax.pmax(peak, 'kv')  17.7 us
    dot_general x2, matrix products, attend(): jnp.einsum('gqd,gkd->gqk', query_group, keyt_rows, preferred_element_type...  11.5 us
    dot_general x2, matrix products, attend(): jnp.einsum('gqk,gkd->gqd', weights_b, valuet_rows, preferred_element_type...  8.52 us
    ppermute x3, starting transfers between devices, grow_blocks(): other = lax.ppermute(pieces, axis, [(i, i ^ bit) for i in range(devices)])  7.33 us
  transfers between devices with their start and end apart: 5, of which 2 were waited for; matrix products, arithmetic and copies ran while one was open for 1% of the time, Pallas kernels for 0%

profile of v1, /device:TPU:0, one launch (start us, length us, event | category | flops | bytes accessed | tf_op | source)
XLA Modules:
  0.0 292.7 jit_solution(5344976120434100693)
XLA Ops:
  7.2 3.0 %collective-permute-start = (bf16[1,256,128]{2,1,0:T(8,128)(2,1)}, bf16[1,256,128]{2,1,0:T(8,128)(2,1)S(1)}, u32[]{:S(2)}, u32[]{:S(2)}) collective-permute-start(bf16[1,256,128]{2,1,0:T(8,128)(2,1)} %bitcast.121), channel_id=1, source_target_pairs={{0,1},{1,0},{2,3},{3,2},{4,5},{5,4},{6,7},{7,6},{8,9},{9,8},{10,11... | collective-permute-start | bytes 196616 | tf_op jit(solution)/shard_map/ppermute | solution.py:21
  10.2 0.8 squeeze.14
  11.1 6.0 %all_gather.16 = bf16[1024,128]{1,0:T(8,128)(2,1)S(1)} all-gather(bf16[256,128]{1,0:T(8,128)(2,1)} %param.12), channel_id=1, replica_groups=mesh['pb'=4,'kv'=8] {'pb'}, dimensions={0}, use_global_device_ids=true | all-gather | bytes 327680 | tf_op jit(solution)/shard_map/all_gather | solution.py:45
  17.1 0.9 broadcast_select_fusion.5
  17.9 1.6 collective-permute-start.1
  19.6 6.0 %all_gather.17 = bf16[1024,128]{1,0:T(8,128)(2,1)S(1)} all-gather(bf16[256,128]{1,0:T(8,128)(2,1)} %param.13), channel_id=1, replica_groups=mesh['pb'=4,'kv'=8] {'pb'}, dimensions={0}, use_global_device_ids=true | all-gather | bytes 327680 | tf_op jit(solution)/shard_map/all_gather | solution.py:46
  25.6 6.0 %all_gather.18 = bf16[1024,128]{1,0:T(8,128)(2,1)S(1)} all-gather(bf16[256,128]{1,0:T(8,128)(2,1)} %param.14), channel_id=1, replica_groups=mesh['pb'=4,'kv'=8] {'pb'}, dimensions={0}, use_global_device_ids=true | all-gather | bytes 327680 | tf_op jit(solution)/shard_map/all_gather | solution.py:47
  31.7 2.7 collective-permute-start.2
  34.3 6.0 %all_gather.19 = bf16[1024,128]{1,0:T(8,128)(2,1)S(1)} all-gather(bf16[256,128]{1,0:T(8,128)(2,1)} %param.15), channel_id=1, replica_groups=mesh['pb'=4,'kv'=8] {'pb'}, dimensions={0}, use_global_device_ids=true | all-gather | bytes 327680 | tf_op jit(solution)/shard_map/all_gather | solution.py:48
  40.3 0.5 broadcast.97
  40.8 1.3 reduce.3
  42.1 0.1 reshape_squeeze.3
  42.2 33.6 %all_gather.15 = bf16[2048,128]{1,0:T(8,128)(2,1)} all-gather(bf16[256,128]{1,0:T(8,128)(2,1)} %param.10), channel_id=1, replica_groups=mesh['pb'=4,'kv'=8] {'kv'}, dimensions={0}, use_global_device_ids=true | all-gather | bytes 589824 | tf_op jit(solution)/shard_map/all_gather | solution.py:41
  75.9 0.9 pad_maximum_fusion
  76.8 57.0 %while.18 = (s32[]{:T(128)}, f32[2,8,128]{2,1,0:T(8,128)S(1)}, f32[2,8,128]{2,1,0:T(8,128)S(1)}, f32[2,8,128,128]{3,2,1,0:T(8,128)}, f32[2,8,128]{2,1,0:T(8,128)...) while((s32[]{:T(128)}, f32[2,8,128]{2,1,0:T(8,128)S(1)}, ...), condition=%wide.region_4.5_spmd, body=%wide.region_0.4_spmd.sunk | while | flops 1634859264 | bytes 101561608 | solution.py:92
  76.9 0.1 reshape.159
  77.0 1.0 gather_fusion
  78.0 3.6 %select_reduce_fusion.2 = (f32[8,128]{1,0:T(8,128)S(1)}, f32[8,128,1024]{2,1,0:T(8,128)}) fusion(pred[8,1024]{1,0:T(8,128)(4,1)S(1)} %broadcast_bitcast_fusion.2, bf16[8,1024,128]{2,1,0:T(8,128)(2,1)S(1)} %bitcast.109, bf16[2,8,128,128]{3,2,1,0:T(8,128)(2,1)} %get-tuple-element.297, s32[]{:T(128)} %get-tuple-element.275), kind=kOutput, calls=%fused_computation.6.clone.1 | convolution fusion | flops 271580160 | bytes 6566400 | tf_op jit(solution)/shard_map/while/body/eval_jaxpr/gqd,gkd->gqk/dot_general | solution.py:71
  81.7 2.7 fusion.66
  84.4 2.2 gather_fusion.1
  86.5 5.7 %fusion.67 = (f32[8,128]{1,0:T(8,128)S(1)}, bf16[8,128,1024]{2,1,0:T(8,128)(2,1)S(1)}) fusion(f32[8,128,1024]{2,1,0:T(8,128)} %fusion.66, bf16[8,1024,128]{2,1,0:T(8,128)(2,1)} %bitcast.115, bf16[2,8,128,128]{3,2,1,0:T(8,128)(2,1)} %get-tuple-element.297, s32[]{:T(128)} %get-tuple-element.275, f32[8,128]{1,0:T(8,128)S(1)} %get-tuple-element.254, ...), kind=kOutput, calls=%fused_computation.70.clone.1 | convolution fusion | flops 276823040 | bytes 12861952 | tf_op jit(solution)/shard_map/while/body/eval_jaxpr/gqd,gkd->gqk/dot_general | solution.py:76
  92.3 2.1 gather_fusion.2
  94.4 3.1 %fusion.70 = f32[8,128,128]{2,1,0:T(8,128)} fusion(bf16[8,1024,128]{2,1,0:T(8,128)(2,1)} %bitcast.116, bf16[8,128,1024]{2,1,0:T(8,128)(2,1)S(1)} %get-tuple-element.259), kind=kOutput, calls=%fused_computation.9.clone.1 | convolution fusion | flops 268435456 | bytes 4718592 | tf_op jit(solution)/shard_map/while/body/eval_jaxpr/gqk,gkd->gqd/dot_general | solution.py:87
  97.5 0.9 gather_fusion.3
  98.5 4.3 %fusion.71 = f32[2,8,128,128]{3,2,1,0:T(8,128)} fusion(f32[2,8,128,128]{3,2,1,0:T(8,128)} %get-tuple-element.280, s32[]{:T(128)} %get-tuple-element.275, f32[8,128,128]{2,1,0:T(8,128)} %fusion.70, bf16[8,1024,128]{2,1,0:T(8,128)(2,1)S(1)} %bitcast.118, f32[8,128,1024]{2,1,0:T(8,128)} %get-tuple-element.255, f32[8,128]{1,0:T(8,128)S(1)} %get-tuple-element.254, ...), kind=kOutput, calls=%fused_computation.15.clone.1 | convolution fusion | flops 272760832 | bytes 7352832 | tf_op jit(solution)/shard_map/while/body/eval_jaxpr/gqk,gkd->gqd/dot_general | solution.py:89
  102.7 0.4 copy-done.3
  103.1 1.0 fusion.69
  104.1 1.1 fusion.68
  105.5 1.0 gather_fusion
  106.5 3.6 %select_reduce_fusion.2 = (f32[8,128]{1,0:T(8,128)S(1)}, f32[8,128,1024]{2,1,0:T(8,128)}) fusion(pred[8,1024]{1,0:T(8,128)(4,1)S(1)} %broadcast_bitcast_fusion.2, bf16[8,1024,128]{2,1,0:T(8,128)(2,1)S(1)} %bitcast.109, bf16[2,8,128,128]{3,2,1,0:T(8,128)(2,1)} %get-tuple-element.297, s32[]{:T(128)} %get-tuple-element.275), kind=kOutput, calls=%fused_computation.6.clone.1 | convolution fusion | flops 271580160 | bytes 6566400 | tf_op jit(solution)/shard_map/while/body/eval_jaxpr/gqd,gkd->gqk/dot_general | solution.py:71
  110.2 2.7 fusion.66
  112.9 2.2 gather_fusion.1
  115.0 5.7 %fusion.67 = (f32[8,128]{1,0:T(8,128)S(1)}, bf16[8,128,1024]{2,1,0:T(8,128)(2,1)S(1)}) fusion(f32[8,128,1024]{2,1,0:T(8,128)} %fusion.66, bf16[8,1024,128]{2,1,0:T(8,128)(2,1)} %bitcast.115, bf16[2,8,128,128]{3,2,1,0:T(8,128)(2,1)} %get-tuple-element.297, s32[]{:T(128)} %get-tuple-element.275, f32[8,128]{1,0:T(8,128)S(1)} %get-tuple-element.254, ...), kind=kOutput, calls=%fused_computation.70.clone.1 | convolution fusion | flops 276823040 | bytes 12861952 | tf_op jit(solution)/shard_map/while/body/eval_jaxpr/gqd,gkd->gqk/dot_general | solution.py:76
  120.8 2.1 gather_fusion.2
  122.9 3.1 %fusion.70 = f32[8,128,128]{2,1,0:T(8,128)} fusion(bf16[8,1024,128]{2,1,0:T(8,128)(2,1)} %bitcast.116, bf16[8,128,1024]{2,1,0:T(8,128)(2,1)S(1)} %get-tuple-element.259), kind=kOutput, calls=%fused_computation.9.clone.1 | convolution fusion | flops 268435456 | bytes 4718592 | tf_op jit(solution)/shard_map/while/body/eval_jaxpr/gqk,gkd->gqd/dot_general | solution.py:87
  126.0 0.9 gather_fusion.3
  127.0 4.3 %fusion.71 = f32[2,8,128,128]{3,2,1,0:T(8,128)} fusion(f32[2,8,128,128]{3,2,1,0:T(8,128)} %get-tuple-element.280, s32[]{:T(128)} %get-tuple-element.275, f32[8,128,128]{2,1,0:T(8,128)} %fusion.70, bf16[8,1024,128]{2,1,0:T(8,128)(2,1)S(1)} %bitcast.118, f32[8,128,1024]{2,1,0:T(8,128)} %get-tuple-element.255, f32[8,128]{1,0:T(8,128)S(1)} %get-tuple-element.254, ...), kind=kOutput, calls=%fused_computation.15.clone.1 | convolution fusion | flops 272760832 | bytes 7352832 | tf_op jit(solution)/shard_map/while/body/eval_jaxpr/gqk,gkd->gqd/dot_general | solution.py:89
  131.2 0.4 copy-done.3
  131.6 1.0 fusion.69
  132.6 1.1 fusion.68
  133.8 17.7 %pmax.7 = f32[2048]{0:T(1024)S(1)} all-reduce(f32[2048]{0:T(1024)S(1)} %bitcast.122), channel_id=1, replica_groups=mesh['pb'=4,'kv'=8] {'kv'}, use_global_device_ids=true, to_apply=%region_5.6 | all-reduce | flops 2048 | bytes 16384 | tf_op jit(solution)/shard_map/pmax | solution.py:107
  151.5 3.2 %bitcast_multiply_fusion = (f32[2048,128]{1,0:T(8,128)}, f32[2048,128]{1,0:T(8,128)}) fusion(f32[2,8,128,128]{3,2,1,0:T(8,128)} %get-tuple-element.81, f32[2048]{0:T(1024)S(1)} %get-tuple-element.144, f32[2,8,128,128]{3,2,1,0:T(8,128)} %get-tuple-element.78), kind=kLoop, calls=%fused_computation.42 | loop fusion | flops 524288 | bytes 4202496 | tf_op jit(solution)/shard_map/mul | solution.py:113
  154.8 0.7 reduce-scatter.5.cloned.1.call-update
  155.5 0.6 dynamic-slice
  156.7 34.9 %all-reduce.2 = (f32[2048]{0:T(1024)S(1)}, f32[2048]{0:T(1024)S(1)}) all-reduce(f32[2048]{0:T(1024)S(1)} %bitcast_multiply_fusion.3, f32[2048]{0:T(1024)S(1)} %get-tuple-element.143), channel_id=3, replica_groups=mesh['pb'=4,'kv'=8] {'kv'}, use_global_device_ids=true, to_apply=%region_7.8.clone | all-reduce | flops 4096 | bytes 32768
  191.7 25.9 %reduce-scatter.3.cloned.1.call-done = f32[256,128]{1,0:T(8,128)} async-done(((f32[2048,128]{1,0:T(8,128)}), f32[256,128]{1,0:T(8,128)}) %reduce-scatter.3.cloned.1.call-update) | async-done | bytes 131088 | tf_op jit(solution)/shard_map/reduce_scatter | solution.py:111
  217.6 66.5 %reduce-scatter.5.cloned.1.call-done = f32[256,128]{1,0:T(8,128)} async-done(((f32[2048,128]{1,0:T(8,128)}), f32[256,128]{1,0:T(8,128)}) %reduce-scatter.5.cloned.1.call-update) | async-done | bytes 131088 | tf_op jit(solution)/shard_map/reduce_scatter | solution.py:113
  284.1 1.7 subtract_convert_fusion
  (58 shorter events, 0.9 us)
Async XLA Ops:
  7.2 210.4 %reduce-scatter.3.cloned.1.call-start = ((), (), s32[]{:S(2)}) async-start(), calls=%async_computation.2 | async-start | bytes 1179648 | tf_op jit(solution)/shard_map/reduce_scatter | solution.py:111
  7.2 9.9 %collective-permute-start = (bf16[1,256,128]{2,1,0:T(8,128)(2,1)}, bf16[1,256,128]{2,1,0:T(8,128)(2,1)S(1)}, u32[]{:S(2)}, u32[]{:S(2)}) collective-permute-start(bf16[1,256,128]{2,1,0:T(8,128)(2,1)} %bitcast.121), channel_id=1, source_target_pairs={{0,1},{1,0},{2,3},{3,2},{4,5},{5,4},{6,7},{7,6},{8,9},{9,8},{10,11... | collective-permute-start | bytes 196616 | tf_op jit(solution)/shard_map/ppermute | solution.py:21
  17.9 13.7 %collective-permute-start.1 = (bf16[2,256,128]{2,1,0:T(8,128)(2,1)S(1)}, bf16[2,256,128]{2,1,0:T(8,128)(2,1)S(1)}, u32[]{:S(2)}, u32[]{:S(2)}) collective-permute-start(bf16[2,256,128]{2,1,0:T(8,128)(2,1)S(1)} %pad_maximum_fusion.2), channel_id=1, source_target_pairs={{0,2},{1,3},{2,0},{3,1},{4,6},{5,7},{6,4},{7,5},{8,10},{9,11},{10,... | collective-permute-start | bytes 393224 | tf_op jit(solution)/shard_map/ppermute | solution.py:21
  31.7 44.2 %collective-permute-start.2 = (bf16[4,256,128]{2,1,0:T(8,128)(2,1)S(1)}, bf16[4,256,128]{2,1,0:T(8,128)(2,1)S(1)}, u32[]{:S(2)}, u32[]{:S(2)}) collective-permute-start(bf16[4,256,128]{2,1,0:T(8,128)(2,1)S(1)} %pad_maximum_fusion.1), channel_id=1, source_target_pairs={{0,4},{1,5},{2,6},{3,7},{4,0},{5,1},{6,2},{7,3},{8,12},{9,13},{10,... | collective-permute-start | bytes 786440 | tf_op jit(solution)/shard_map/ppermute | solution.py:21
  77.9 3.8 %copy-start.2 = (bf16[2,8,128,128]{3,2,1,0:T(8,128)(2,1)S(1)}, bf16[2,8,128,128]{3,2,1,0:T(8,128)(2,1)}, u32[]{:S(2)}) copy-start(bf16[2,8,128,128]{3,2,1,0:T(8,128)(2,1)} %get-tuple-element.301) | copy-start | bytes 1572868 | tf_op jit(solution)/shard_map/while
  98.4 4.3 %copy-start = (f32[8,128,1024]{2,1,0:T(8,128)S(1)}, f32[8,128,1024]{2,1,0:T(8,128)}, u32[]{:S(2)}) copy-start(f32[8,128,1024]{2,1,0:T(8,128)} %get-tuple-element.255) | copy-start | bytes 12582916 | tf_op jit(solution)/shard_map/while
  98.5 4.3 %copy-start.1 = (bf16[64,128,128]{2,1,0:T(8,128)(2,1)S(1)}, bf16[64,128,128]{2,1,0:T(8,128)(2,1)}, u32[]{:S(2)}) copy-start(bf16[64,128,128]{2,1,0:T(8,128)(2,1)} %gather_fusion.2) | copy-start | bytes 6291460 | tf_op jit(solution)/shard_map/while
  98.5 4.7 %copy-start.3 = (f32[2,8,128,128]{3,2,1,0:T(8,128)S(1)}, f32[2,8,128,128]{3,2,1,0:T(8,128)}, u32[]{:S(2)}) copy-start(f32[2,8,128,128]{3,2,1,0:T(8,128)} %get-tuple-element.278) | copy-start | bytes 3145732 | tf_op jit(solution)/shard_map/while
  104.1 1.1 copy-start.4
  106.4 3.8 %copy-start.2 = (bf16[2,8,128,128]{3,2,1,0:T(8,128)(2,1)S(1)}, bf16[2,8,128,128]{3,2,1,0:T(8,128)(2,1)}, u32[]{:S(2)}) copy-start(bf16[2,8,128,128]{3,2,1,0:T(8,128)(2,1)} %get-tuple-element.301) | copy-start | bytes 1572868 | tf_op jit(solution)/shard_map/while
  127.0 4.3 %copy-start = (f32[8,128,1024]{2,1,0:T(8,128)S(1)}, f32[8,128,1024]{2,1,0:T(8,128)}, u32[]{:S(2)}) copy-start(f32[8,128,1024]{2,1,0:T(8,128)} %get-tuple-element.255) | copy-start | bytes 12582916 | tf_op jit(solution)/shard_map/while
  127.0 4.3 %copy-start.1 = (bf16[64,128,128]{2,1,0:T(8,128)(2,1)S(1)}, bf16[64,128,128]{2,1,0:T(8,128)(2,1)}, u32[]{:S(2)}) copy-start(bf16[64,128,128]{2,1,0:T(8,128)(2,1)} %gather_fusion.2) | copy-start | bytes 6291460 | tf_op jit(solution)/shard_map/while
  127.0 4.7 %copy-start.3 = (f32[2,8,128,128]{3,2,1,0:T(8,128)S(1)}, f32[2,8,128,128]{3,2,1,0:T(8,128)}, u32[]{:S(2)}) copy-start(f32[2,8,128,128]{3,2,1,0:T(8,128)} %get-tuple-element.278) | copy-start | bytes 3145732 | tf_op jit(solution)/shard_map/while
  132.6 1.1 copy-start.4
  133.8 21.7 %copy-start.5 = (u32[32]{0:T(128)S(1)}, u32[32]{0:T(128)}, u32[]{:S(2)}) copy-start(u32[32]{0:T(128)} %constant.81) | copy-start | bytes 388
  154.7 129.4 %reduce-scatter.5.cloned.1.call-start = ((), (), s32[]{:S(2)}) async-start(), calls=%async_computation.3 | async-start | bytes 1179648 | tf_op jit(solution)/shard_map/reduce_scatter | solution.py:113
Sparse Core Ops, SparseCore 0:
  154.8 62.6 reduce-scatter.2
  221.0 63.0 reduce-scatter.4
